TPU v7x, 32 devices: a whole 2x2x4 slice. The times are simulated.
32 devices in a mesh: groups: 2 (over x), dp: 16 (over z, y, core).
Axes of the slice: x: 2, y: 2, z: 4, core: 2. Of those that a mesh axis runs over, the one named last changes fastest.
Arguments:
- activations: bfloat16 [12288, 16384], P(('groups', 'dp')), parts along dimension 0, may hold values from -18 to 18
- labels: int32 [12288], P(('groups', 'dp')), parts along dimension 0, may hold values from 0 to 63, as said below
- counts: int32 [12288], P(('groups', 'dp')), parts along dimension 0, may hold values from 1 to 4
Outputs:
- solution: float32 [32768, 64], P(('groups', 'dp')), parts along dimension 0
- residual: float32 [32768, 64], P(('groups', 'dp')), parts along dimension 0
There are 2 independent parts, one for each index of `groups`. A program takes and returns all parts, laid end to end along the dimension named above; each array names one. Nothing has to cross between parts.
Inputs may be any that keep to these rules, and one draw needn't show every extreme that they name: `labels`: concept index of each row; every concept of 0 to 63 names at least one row. `counts`: integer sample weight of each row.
All inputs are finite; a program needn't handle non-finite values.
Results may differ from a plain program's by a relative error of at most 0.012.
The roundings to bfloat16 on the way count: a program that leaves them out, or rounds other values in their place, can miss the bound.
Values may be sent and summed in bfloat16 or wider, within the bound.
No kernel may reach another device: no remote copies, remote signals or barrier semaphores. Data moves between devices by JAX's collectives and lax.ppermute only.
A program may use at most 64 MiB of HBM per device.

v0:
```python
import jax
import jax.numpy as jnp
from jax import lax
from jax.sharding import PartitionSpec as P

K = 64
ITERS = 2
RIDGE = 0.1


def precise(left_side, right_side):
    return jnp.dot(
        left_side, right_side, precision=lax.Precision.HIGHEST, preferred_element_type=jnp.float32
    )


def symmetric(matrix):
    return 0.5 * (matrix + matrix.T)


def solve_positive(matrix, target):
    return jax.scipy.linalg.cho_solve((jnp.linalg.cholesky(matrix), True), target)


def contract_rows(left_side, right_side):
    return lax.dot_general(
        left_side, right_side, (((0,), (0,)), ((), ())), preferred_element_type=jnp.float32
    )


def per_device(activations, labels, counts):
    weights = counts.astype(jnp.float32)
    classes = jnp.arange(K, dtype=jnp.int32)
    member_full = jnp.where(labels[:, None] == classes[None, :], weights[:, None], jnp.float32(0.0))
    local_weight = jnp.sum(member_full, axis=0)
    member = member_full.astype(jnp.bfloat16)
    class_sums = lax.psum_scatter(
        contract_rows(activations, member), "dp", scatter_dimension=0, tiled=True
    )
    class_weight = lax.psum(local_weight, "dp")
    total_weight = jnp.sum(class_weight)
    class_means = class_sums / class_weight[None, :]
    mean_diff = class_means * jnp.sqrt(class_weight)[None, :]
    solution = jnp.zeros_like(mean_diff)
    residual = mean_diff
    direction = mean_diff
    current = symmetric(lax.psum(precise(residual.T, residual), "dp"))
    for iteration in range(ITERS):
        probed = jnp.dot(
            activations,
            lax.all_gather(direction.astype(jnp.bfloat16), "dp", axis=0, tiled=True),
            preferred_element_type=jnp.float32,
        )
        weighted = (weights[:, None] * probed).astype(jnp.bfloat16)
        panel = lax.psum_scatter(
            contract_rows(activations, weighted), "dp", scatter_dimension=0, tiled=True
        )
        cross, along_panel, along_along = lax.psum(
            (
                precise(class_means.T, direction),
                precise(direction.T, panel),
                precise(direction.T, direction),
            ),
            "dp",
        )
        scaled = class_weight[:, None] * cross
        curvature = symmetric(
            (along_panel - precise(cross.T, scaled)) / total_weight + RIDGE * along_along
        )
        step_alpha = solve_positive(curvature, current)
        image = (panel - precise(class_means, scaled)) / total_weight + RIDGE * direction
        solution = solution + precise(direction, step_alpha)
        residual = residual - precise(image, step_alpha)
        renewed = current
        if iteration + 1 < ITERS:
            renewed = symmetric(lax.psum(precise(residual.T, residual), "dp"))
        if iteration + 1 < ITERS:
            step_beta = solve_positive(current, renewed)
            direction = residual + precise(direction, step_beta)
            current = renewed
    return (solution, residual)


def solution(mesh):
    in_specs = (P(("groups", "dp"), None), P(("groups", "dp")), P(("groups", "dp")))
    out_specs = (P(("groups", "dp"), None), P(("groups", "dp"), None))
    return jax.shard_map(
        per_device, mesh=mesh, in_specs=in_specs, out_specs=out_specs, check_vma=False
    )
```

profile of v0, /device:TPU:0, one launch (start us, length us, event | category | flops | bytes accessed | tf_op | source)
XLA Modules:
  0.0 587.8 jit_solution(6999212861251710433)
XLA Ops:
  7.2 0.7 convert_element_type.20
  7.9 8.9 %convolution_bitcast_fusion.2 = f32[16384,64]{0,1:T(8,128)} fusion(bf16[384,16384]{1,0:T(8,128)(2,1)} %param.6, f32[384]{0:T(512)S(1)} %convert_element_type.20, s32[384]{0:T(512)} %param.7), kind=kOutput, calls=%fused_computation.2 | convolution fusion | flops 805355520 | bytes 16780288 | tf_op jit(solution)/shard_map/dot_general | solution.py:26
  17.0 35.0 %psum.59 = f32[64]{0:T(128)S(1)} all-reduce(f32[64]{0:T(128)S(1)} %select_reduce_fusion), channel_id=1, replica_groups=mesh['groups'=2,'dp'=16] {'dp'}, use_global_device_ids=true, to_apply=%region_2.3 | all-reduce | flops 64 | bytes 512 | tf_op jit(solution)/shard_map/psum | solution.py:40
  52.0 0.6 fusion.62
  52.6 39.5 %reduce-scatter.4.cloned.1.call-done = f32[1024,64]{0,1:T(8,128)} async-done(((f32[16384,64]{0,1:T(8,128)}), f32[1024,64]{0,1:T(8,128)}) %reduce-scatter.4.cloned.1.call-update) | async-done | bytes 262160 | tf_op jit(solution)/shard_map/reduce_scatter | solution.py:37
  92.1 1.7 multiply_convert_fusion
  93.9 41.7 %all-gather.3.cloned.1.call-done = bf16[16384,64]{0,1:T(8,128)(2,1)} async-done(((bf16[1024,64]{0,1:T(8,128)(2,1)}), bf16[16384,64]{0,1:T(8,128)(2,1)}) %all-gather.3.cloned.1.call-update) | async-done | bytes 2097168 | tf_op jit(solution)/shard_map/all_gather | solution.py:51
  135.5 18.5 %convolution_bitcast_fusion.1 = f32[16384,64]{0,1:T(8,128)} fusion(bf16[384,16384]{1,0:T(8,128)(2,1)} %param.6, bf16[16384,64]{0,1:T(8,128)(2,1)} %all-gather.3.cloned.1.call-done, f32[384]{0:T(512)S(1)} %convert_element_type.20), kind=kOutput, calls=%fused_computation.1 | convolution fusion | flops 1610661888 | bytes 18875904 | tf_op jit(solution)/shard_map/dot_general | solution.py:26
  154.1 0.5 fusion.13
  154.5 0.5 fusion.15
  155.0 70.3 %reduce-scatter.6.cloned.1.call-done = f32[1024,64]{0,1:T(8,128)} async-done(((f32[16384,64]{0,1:T(8,128)}), f32[1024,64]{0,1:T(8,128)}) %reduce-scatter.6.cloned.1.call-update) | async-done | bytes 262160 | tf_op jit(solution)/shard_map/reduce_scatter | solution.py:55
  225.3 1.4 fusion.17
  226.7 59.2 %all-reduce.1 = (f32[64,64]{1,0:T(8,128)S(1)}, f32[64,64]{1,0:T(8,128)S(1)}, f32[64,64]{1,0:T(8,128)S(1)}) all-reduce(f32[64,64]{1,0:T(8,128)S(1)} %fusion.13, f32[64,64]{1,0:T(8,128)S(1)} %fusion.17, f32[64,64]{1,0:T(8,128)S(1)} %fusion.15), channel_id=1, replica_groups=mesh['groups'=2,'dp'=16] {'dp'}, use_global_device_ids=true, to_apply=%region_7.8 | all-reduce | flops 12288 | bytes 98304 | tf_op jit(solution)/shard_map/psum | solution.py:58
  286.1 5.8 cholesky.70
  292.0 0.6 compare_reduce_fusion.1
  292.6 0.7 fusion.32
  293.3 4.9 custom-call.10
  298.2 0.9 fusion.9
  299.4 5.9 cholesky.59
  305.3 0.6 compare_reduce_fusion.2
  305.9 0.7 fusion.31
  306.6 4.9 custom-call.9
  311.5 0.2 fusion.48
  311.9 2.1 fusion.3
  314.0 0.4 convolution_subtract_fusion.2
  314.4 0.4 fusion.64
  314.8 57.6 %psum.63 = f32[64,64]{1,0:T(8,128)S(1)} all-reduce(f32[64,64]{1,0:T(8,128)S(1)} %fusion.64), channel_id=1, replica_groups=mesh['groups'=2,'dp'=16] {'dp'}, use_global_device_ids=true, to_apply=%region_10.13 | all-reduce | flops 4096 | bytes 32768 | tf_op jit(solution)/shard_map/psum | solution.py:76
  372.5 0.2 fusion.42
  372.8 0.2 fusion.40
  372.9 1.1 fusion.63
  374.1 0.3 reduce-scatter.8.cloned.1.call-start
  374.3 38.6 %all-gather.5.cloned.1.call-done = bf16[16384,64]{0,1:T(8,128)(2,1)} async-done(((bf16[1024,64]{0,1:T(8,128)(2,1)}), bf16[16384,64]{0,1:T(8,128)(2,1)}) %all-gather.5.cloned.1.call-update) | async-done | bytes 2097168 | tf_op jit(solution)/shard_map/all_gather | solution.py:51
  412.9 18.5 %convolution_bitcast_fusion = f32[16384,64]{0,1:T(8,128)} fusion(bf16[384,16384]{1,0:T(8,128)(2,1)} %param.6, bf16[16384,64]{0,1:T(8,128)(2,1)} %all-gather.5.cloned.1.call-done, f32[384]{0:T(512)S(1)} %convert_element_type.20), kind=kOutput, calls=%fused_computation | convolution fusion | flops 1610661888 | bytes 18875904 | tf_op jit(solution)/shard_map/dot_general | solution.py:26
  431.4 0.4 fusion.66
  431.7 0.4 fusion.61
  432.2 0.5 fusion.11
  432.6 70.1 %reduce-scatter.8.cloned.1.call-done = f32[1024,64]{0,1:T(8,128)} async-done(((f32[16384,64]{0,1:T(8,128)}), f32[1024,64]{0,1:T(8,128)}) %reduce-scatter.8.cloned.1.call-update) | async-done | bytes 262160 | tf_op jit(solution)/shard_map/reduce_scatter | solution.py:55
  502.8 1.3 fusion.65
  504.1 59.1 %all-reduce = (f32[64,64]{1,0:T(8,128)S(1)}, f32[64,64]{1,0:T(8,128)S(1)}, f32[64,64]{1,0:T(8,128)S(1)}) all-reduce(f32[64,64]{1,0:T(8,128)S(1)} %fusion.65, f32[64,64]{1,0:T(8,128)S(1)} %fusion.61, f32[64,64]{1,0:T(8,128)S(1)} %fusion.66), channel_id=1, replica_groups=mesh['groups'=2,'dp'=16] {'dp'}, use_global_device_ids=true, to_apply=%region_12.15 | all-reduce | flops 12288 | bytes 98304 | tf_op jit(solution)/shard_map/psum | solution.py:58
  563.2 0.9 fusion.7
  564.4 5.8 cholesky.81
  570.3 0.6 compare_reduce_fusion
  570.9 0.7 fusion.33
  571.6 4.9 custom-call.11
  576.5 0.2 fusion.36
  576.9 2.1 fusion.1
  579.0 1.1 convolution_subtract_fusion
  580.1 1.1 convolution_add_fusion
  (35 shorter events, 1.5 us)
Async XLA Ops:
  7.2 9.7 %copy-start.1 = (s32[384]{0:T(512)S(1)}, s32[384]{0:T(512)}, u32[]{:S(2)}) copy-start(s32[384]{0:T(512)} %param.7) | copy-start | bytes 4612
  7.2 84.9 %reduce-scatter.4.cloned.1.call-start = ((), (), s32[]{:S(2)}) async-start(), calls=%async_computation.3 | async-start | bytes 4456448 | tf_op jit(solution)/shard_map/reduce_scatter | solution.py:37
  16.8 118.7 %all-gather.3.cloned.1.call-start = ((), (), s32[]{:S(2)}) async-start(), calls=%async_computation.4 | async-start | bytes 2228224 | tf_op jit(solution)/shard_map/all_gather | solution.py:51
  93.8 60.3 %copy-start = (f32[1024,64]{0,1:T(8,128)S(1)}, f32[1024,64]{0,1:T(8,128)}, u32[]{:S(2)}) copy-start(f32[1024,64]{0,1:T(8,128)} %reduce-scatter.4.cloned.1.call-done) | copy-start | bytes 786436
  93.8 131.5 %reduce-scatter.6.cloned.1.call-start = ((), (), s32[]{:S(2)}) async-start(), calls=%async_computation.5 | async-start | bytes 4456448 | tf_op jit(solution)/shard_map/reduce_scatter | solution.py:55
  154.0 258.9 %all-gather.5.cloned.1.call-start = ((), (), s32[]{:S(2)}) async-start(), calls=%async_computation.6 | async-start | bytes 2228224 | tf_op jit(solution)/shard_map/all_gather | solution.py:51
  374.1 128.7 %reduce-scatter.8.cloned.1.call-start = ((), (), s32[]{:S(2)}) async-start(), calls=%async_computation.7 | async-start | bytes 4456448 | tf_op jit(solution)/shard_map/reduce_scatter | solution.py:55
Sparse Core Ops, SparseCore 0:
  16.9 75.1 reduce-scatter.3
  95.1 40.4 all-gather.2
  154.1 71.1 reduce-scatter.5
  374.2 38.6 all-gather.4
  431.5 71.2 reduce-scatter.7
where the time goes:
time: 588 us
  waiting for transfers between devices  260 us (44%)
  blocking collectives  211 us (36%)
  matrix products  62 us (11%)
  other arithmetic  39.4 us (7%)
  between operations  14.1 us (2%)
    reduce_scatter x2, waiting for transfers between devices, per_device(): lax.psum_scatter(contract_rows(activations, weighted), 'dp', scatter_dime...  140 us
    psum x2, blocking collectives, per_device(): lax.psum((precise(class_means.T, direction), precise(direction.T, panel),...  118 us
    all_gather x2, waiting for transfers between devices, per_device(): lax.all_gather(direction.astype(jnp.bfloat16), 'dp', axis=0, tiled=True)  80.2 us
    psum x1, blocking collectives, per_device(): renewed = symmetric(lax.psum(precise(residual.T, residual), 'dp'))  57.6 us
    dot_general x3, matrix products, contract_rows(): lax.dot_general(left_side, right_side, (((0,), (0,)), ((), ())), preferre...  45.8 us
    reduce_scatter x1, waiting for transfers between devices, per_device(): lax.psum_scatter(contract_rows(activations, member), 'dp', scatter_dimens...  39.5 us
    psum x1, blocking collectives, per_device(): class_weight = lax.psum(local_weight, 'dp')  35 us
    another operation x9, other arithmetic, solve_positive(): jnp.linalg.cholesky(matrix)  19.6 us
  transfers between devices with their start and end apart: 5, of which 5 were waited for; matrix products, arithmetic and copies ran while one was open for 0% of the time, Pallas kernels for 0%

commit v1 on v0

--- a/solution.py
+++ b/solution.py
@@ -6,6 +6,18 @@
 K = 64
 ITERS = 2
 RIDGE = 0.1
+
+
+def gather_by_bits(x, axis, dim):
+    ways, here = (lax.axis_size(axis), lax.axis_index(axis))
+    grown, reach = (x, 1)
+    while reach < ways:
+        theirs = lax.ppermute(grown, axis, [(d, d ^ reach) for d in range(ways)])
+        mine_first = jnp.concatenate([grown, theirs], axis=dim)
+        theirs_first = jnp.concatenate([theirs, grown], axis=dim)
+        grown = jnp.where(here & reach == 0, mine_first, theirs_first)
+        reach = 2 * reach
+    return grown
 
 
 def precise(left_side, right_side):
@@ -48,7 +60,7 @@
     for iteration in range(ITERS):
         probed = jnp.dot(
             activations,
-            lax.all_gather(direction.astype(jnp.bfloat16), "dp", axis=0, tiled=True),
+            gather_by_bits(direction.astype(jnp.bfloat16), "dp", 0),
             preferred_element_type=jnp.float32,
         )
         weighted = (weights[:, None] * probed).astype(jnp.bfloat16)

time: 588 us -> 642 us (1.092)
  waiting for transfers between devices: 260 us -> 314 us
    ppermute x0 -> x8, waiting for transfers between devices: none -> 136 us  [gather_by_bits(): theirs = lax.ppermute(grown, axis, [(d, d ^ reach) for d in range(ways)])]
    all_gather x2 -> x0, waiting for transfers between devices: 80.2 us -> none  [per_device(): lax.all_gather(direction.astype(jnp.bfloat16), 'dp', axis=0, tiled=True)]
    dot_general x3, matrix products: 45.8 us -> 26.7 us  [contract_rows(): lax.dot_general(left_side, right_side, (((0,), (0,)), ((), ())), preferre...]
    dot_general x0 -> x2, matrix products: none -> 14.8 us  [per_device(): jnp.dot(activations, gather_by_bits(direction.astype(jnp.bfloat16), 'dp',...]
  transfers between devices with their start and end apart: 5 -> 11, of which waited for: 5 -> 11; matrix products, arithmetic and copies ran while one was open for 0% -> 0% of each run, Pallas kernels for 0% -> 0%
where the time goes in v1:
time: 642 us
  waiting for transfers between devices  314 us (49%)
  blocking collectives  211 us (33%)
  matrix products  57.1 us (9%)
  other arithmetic  39.6 us (6%)
  between operations  14.1 us (2%)
    reduce_scatter x2, waiting for transfers between devices, per_device(): lax.psum_scatter(contract_rows(activations, weighted), 'dp', scatter_dime...  139 us
    ppermute x8, waiting for transfers between devices, gather_by_bits(): theirs = lax.ppermute(grown, axis, [(d, d ^ reach) for d in range(ways)])  136 us
    psum x2, blocking collectives, per_device(): lax.psum((precise(class_means.T, direction), precise(direction.T, panel),...  118 us
    psum x1, blocking collectives, per_device(): renewed = symmetric(lax.psum(precise(residual.T, residual), 'dp'))  57.6 us
    reduce_scatter x1, waiting for transfers between devices, per_device(): lax.psum_scatter(contract_rows(activations, member), 'dp', scatter_dimens...  38.8 us
    psum x1, blocking collectives, per_device(): class_weight = lax.psum(local_weight, 'dp')  35 us
    dot_general x3, matrix products, contract_rows(): lax.dot_general(left_side, right_side, (((0,), (0,)), ((), ())), preferre...  26.7 us
    another operation x9, other arithmetic, solve_positive(): jnp.linalg.cholesky(matrix)  19.6 us
  transfers between devices with their start and end apart: 11, of which 11 were waited for; matrix products, arithmetic and copies ran while one was open for 0% of the time, Pallas kernels for 0%

profile of v1, /device:TPU:0, one launch (start us, length us, event | category | flops | bytes accessed | tf_op | source)
XLA Modules:
  0.0 641.7 jit_solution(11604604781815763886)
XLA Ops:
  7.2 0.7 convert_element_type.20
  7.9 8.8 %convolution_bitcast_fusion.2 = f32[16384,64]{0,1:T(8,128)} fusion(bf16[384,16384]{1,0:T(8,128)(2,1)} %param.6, f32[384]{0:T(512)S(1)} %convert_element_type.20, s32[384]{0:T(512)} %param.7), kind=kOutput, calls=%fused_computation.2 | convolution fusion | flops 805355520 | bytes 16780288 | tf_op jit(solution)/shard_map/dot_general | solution.py:38
  16.8 0.6 copy-done.1
  17.5 35.0 %psum.59 = f32[64]{0:T(128)S(1)} all-reduce(f32[64]{0:T(128)S(1)} %select_reduce_fusion), channel_id=1, replica_groups=mesh['groups'=2,'dp'=16] {'dp'}, use_global_device_ids=true, to_apply=%region_2.3 | all-reduce | flops 64 | bytes 512 | tf_op jit(solution)/shard_map/psum | solution.py:52
  52.6 0.6 fusion.80
  53.2 38.8 %reduce-scatter.4.cloned.1.call-done = f32[1024,64]{0,1:T(8,128)} async-done(((f32[16384,64]{0,1:T(8,128)}), f32[1024,64]{0,1:T(8,128)}) %reduce-scatter.4.cloned.1.call-update) | async-done | bytes 262160 | tf_op jit(solution)/shard_map/reduce_scatter | solution.py:49
  92.0 1.0 multiply_convert_fusion
  93.1 1.3 collective-permute-done
  94.5 0.9 collective-permute-start.1
  95.4 7.5 %collective-permute-done.1 = bf16[2048,64]{0,1:T(8,128)(2,1)S(1)} collective-permute-done((bf16[2048,64]{0,1:T(8,128)(2,1)S(1)}, bf16[2048,64]{0,1:T(8,128)(2,1)S(1)}, u32[]{:S(2)}, u32[]{:S(2)}) %collective-permute-start.1) | collective-permute-done | bytes 262176 | tf_op jit(solution)/shard_map/ppermute | solution.py:15
  103.1 1.0 collective-permute-start.2
  104.0 12.3 %collective-permute-done.2 = bf16[4096,64]{0,1:T(8,128)(2,1)S(1)} collective-permute-done((bf16[4096,64]{0,1:T(8,128)(2,1)S(1)}, bf16[4096,64]{0,1:T(8,128)(2,1)S(1)}, u32[]{:S(2)}, u32[]{:S(2)}) %collective-permute-start.2) | collective-permute-done | bytes 524320 | tf_op jit(solution)/shard_map/ppermute | solution.py:15
  116.5 1.6 collective-permute-start.3
  118.1 45.3 %collective-permute-done.3 = bf16[8192,64]{0,1:T(8,128)(2,1)S(1)} collective-permute-done((bf16[8192,64]{0,1:T(8,128)(2,1)S(1)}, bf16[8192,64]{0,1:T(8,128)(2,1)S(1)}, u32[]{:S(2)}, u32[]{:S(2)}) %collective-permute-start.3) | collective-permute-done | bytes 1048608 | tf_op jit(solution)/shard_map/ppermute | solution.py:15
  163.4 7.5 %fusion.20 = bf16[64,384]{1,0:T(8,128)(2,1)S(1)} fusion(bf16[384,16384]{1,0:T(8,128)(2,1)} %param.6, bf16[8192,64]{0,1:T(8,128)(2,1)S(1)} %collective-permute-done.3, bf16[8192,64]{0,1:T(8,128)(2,1)S(1)} %maximum_select_fusion.12, pred[]{:T(512)S(6)} %eq.32, f32[384]{0:T(512)S(1)} %convert_element_type.20), kind=kOutput, calls=%fused_computation.31 | convolution fusion | flops 814792704 | bytes 14730753 | tf_op jit(solution)/shard_map/dot_general | solution.py:61
  170.9 8.9 %convolution_bitcast_fusion.1 = f32[16384,64]{0,1:T(8,128)} fusion(bf16[64,384]{1,0:T(8,128)(2,1)S(1)} %fusion.20, bf16[384,16384]{1,0:T(8,128)(2,1)} %param.6), kind=kOutput, calls=%fused_computation.1 | convolution fusion | flops 805306368 | bytes 16826368 | tf_op jit(solution)/shard_map/dot_general | solution.py:38
  179.9 0.9 copy-done
  181.7 69.5 %reduce-scatter.6.cloned.1.call-done = f32[1024,64]{0,1:T(8,128)} async-done(((f32[16384,64]{0,1:T(8,128)}), f32[1024,64]{0,1:T(8,128)}) %reduce-scatter.6.cloned.1.call-update) | async-done | bytes 262160 | tf_op jit(solution)/shard_map/reduce_scatter | solution.py:67
  251.2 1.4 fusion.33
  252.6 59.2 %all-reduce.1 = (f32[64,64]{1,0:T(8,128)S(1)}, f32[64,64]{1,0:T(8,128)S(1)}, f32[64,64]{1,0:T(8,128)S(1)}) all-reduce(f32[64,64]{1,0:T(8,128)S(1)} %fusion.29, f32[64,64]{1,0:T(8,128)S(1)} %fusion.33, f32[64,64]{1,0:T(8,128)S(1)} %fusion.31), channel_id=1, replica_groups=mesh['groups'=2,'dp'=16] {'dp'}, use_global_device_ids=true, to_apply=%region_7.8 | all-reduce | flops 12288 | bytes 98304 | tf_op jit(solution)/shard_map/psum | solution.py:70
  312.0 5.8 cholesky.70
  317.9 0.6 compare_reduce_fusion.1
  318.6 0.7 fusion.48
  319.2 4.9 custom-call.10
  324.1 0.9 fusion.25
  325.3 5.9 cholesky.59
  331.2 0.6 compare_reduce_fusion.2
  331.8 0.7 fusion.47
  332.5 4.9 custom-call.9
  337.8 2.1 fusion.17
  340.7 57.6 %psum.63 = f32[64,64]{1,0:T(8,128)S(1)} all-reduce(f32[64,64]{1,0:T(8,128)S(1)} %fusion.82), channel_id=1, replica_groups=mesh['groups'=2,'dp'=16] {'dp'}, use_global_device_ids=true, to_apply=%region_10.13 | all-reduce | flops 4096 | bytes 32768 | tf_op jit(solution)/shard_map/psum | solution.py:88
  399.4 1.3 collective-permute-done.4
  400.9 8.3 %collective-permute-done.5 = bf16[2048,64]{0,1:T(8,128)(2,1)S(1)} collective-permute-done((bf16[2048,64]{0,1:T(8,128)(2,1)S(1)}, bf16[2048,64]{0,1:T(8,128)(2,1)S(1)}, u32[]{:S(2)}, u32[]{:S(2)}) %collective-permute-start.5) | collective-permute-done | bytes 262176 | tf_op jit(solution)/shard_map/ppermute | solution.py:15
  409.4 13.1 %collective-permute-done.6 = bf16[4096,64]{0,1:T(8,128)(2,1)S(1)} collective-permute-done((bf16[4096,64]{0,1:T(8,128)(2,1)S(1)}, bf16[4096,64]{0,1:T(8,128)(2,1)S(1)}, u32[]{:S(2)}, u32[]{:S(2)}) %collective-permute-start.6) | collective-permute-done | bytes 524320 | tf_op jit(solution)/shard_map/ppermute | solution.py:15
  422.9 46.8 %collective-permute-done.7 = bf16[8192,64]{0,1:T(8,128)(2,1)S(1)} collective-permute-done((bf16[8192,64]{0,1:T(8,128)(2,1)S(1)}, bf16[8192,64]{0,1:T(8,128)(2,1)S(1)}, u32[]{:S(2)}, u32[]{:S(2)}) %collective-permute-start.7) | collective-permute-done | bytes 1048608 | tf_op jit(solution)/shard_map/ppermute | solution.py:15
  469.7 7.4 %fusion.21 = bf16[64,384]{1,0:T(8,128)(2,1)S(1)} fusion(bf16[384,16384]{1,0:T(8,128)(2,1)} %param.6, bf16[8192,64]{0,1:T(8,128)(2,1)S(1)} %collective-permute-done.7, bf16[8192,64]{0,1:T(8,128)(2,1)S(1)} %maximum_select_fusion.13, pred[]{:T(512)S(6)} %eq.32, f32[384]{0:T(512)S(1)} %convert_element_type.20), kind=kOutput, calls=%fused_computation.32 | convolution fusion | flops 814792704 | bytes 14730753 | tf_op jit(solution)/shard_map/dot_general | solution.py:61
  477.1 8.9 %convolution_bitcast_fusion = f32[16384,64]{0,1:T(8,128)} fusion(bf16[64,384]{1,0:T(8,128)(2,1)S(1)} %fusion.21, bf16[384,16384]{1,0:T(8,128)(2,1)} %param.6), kind=kOutput, calls=%fused_computation | convolution fusion | flops 805306368 | bytes 16826368 | tf_op jit(solution)/shard_map/dot_general | solution.py:38
  487.3 69.3 %reduce-scatter.8.cloned.1.call-done = f32[1024,64]{0,1:T(8,128)} async-done(((f32[16384,64]{0,1:T(8,128)}), f32[1024,64]{0,1:T(8,128)}) %reduce-scatter.8.cloned.1.call-update) | async-done | bytes 262160 | tf_op jit(solution)/shard_map/reduce_scatter | solution.py:67
  556.6 1.3 fusion.83
  557.9 59.2 %all-reduce = (f32[64,64]{1,0:T(8,128)S(1)}, f32[64,64]{1,0:T(8,128)S(1)}, f32[64,64]{1,0:T(8,128)S(1)}) all-reduce(f32[64,64]{1,0:T(8,128)S(1)} %fusion.83, f32[64,64]{1,0:T(8,128)S(1)} %fusion.79, f32[64,64]{1,0:T(8,128)S(1)} %fusion.84), channel_id=1, replica_groups=mesh['groups'=2,'dp'=16] {'dp'}, use_global_device_ids=true, to_apply=%region_12.15 | all-reduce | flops 12288 | bytes 98304 | tf_op jit(solution)/shard_map/psum | solution.py:70
  617.1 0.9 fusion.23
  618.3 5.8 cholesky.81
  624.2 0.6 compare_reduce_fusion
  624.8 0.7 fusion.49
  625.5 4.9 custom-call.11
  630.8 2.1 fusion.15
  632.9 1.1 convolution_subtract_fusion
  634.0 1.1 convolution_add_fusion
  (53 shorter events, 7.0 us)
Async XLA Ops:
  7.2 84.8 %reduce-scatter.4.cloned.1.call-start = ((), (), s32[]{:S(2)}) async-start(), calls=%async_computation.3 | async-start | bytes 4456448 | tf_op jit(solution)/shard_map/reduce_scatter | solution.py:49
  16.7 0.7 copy-start.1
  16.8 234.4 %reduce-scatter.6.cloned.1.call-start = ((), (), s32[]{:S(2)}) async-start(), calls=%async_computation.4 | async-start | bytes 4456448 | tf_op jit(solution)/shard_map/reduce_scatter | solution.py:67
  93.0 1.4 collective-permute-start
  94.5 8.4 %collective-permute-start.1 = (bf16[2048,64]{0,1:T(8,128)(2,1)S(1)}, bf16[2048,64]{0,1:T(8,128)(2,1)S(1)}, u32[]{:S(2)}, u32[]{:S(2)}) collective-permute-start(bf16[2048,64]{0,1:T(8,128)(2,1)S(1)} %maximum_select_fusion.16), channel_id=1, source_target_pairs={{0,2},{1,3},{2,0},{3,1},{4,6},{5,7},{6,4},{7,5},{8,10},{9,11},{10,... | collective-permute-start | bytes 786440 | tf_op jit(solution)/shard_map/ppermute | solution.py:15
  103.1 13.2 %collective-permute-start.2 = (bf16[4096,64]{0,1:T(8,128)(2,1)S(1)}, bf16[4096,64]{0,1:T(8,128)(2,1)S(1)}, u32[]{:S(2)}, u32[]{:S(2)}) collective-permute-start(bf16[4096,64]{0,1:T(8,128)(2,1)S(1)} %maximum_select_fusion.14), channel_id=1, source_target_pairs={{0,4},{1,5},{2,6},{3,7},{4,0},{5,1},{6,2},{7,3},{8,12},{9,13},{10,... | collective-permute-start | bytes 1572872 | tf_op jit(solution)/shard_map/ppermute | solution.py:15
  116.5 46.9 %collective-permute-start.3 = (bf16[8192,64]{0,1:T(8,128)(2,1)S(1)}, bf16[8192,64]{0,1:T(8,128)(2,1)S(1)}, u32[]{:S(2)}, u32[]{:S(2)}) collective-permute-start(bf16[8192,64]{0,1:T(8,128)(2,1)S(1)} %maximum_select_fusion.12), channel_id=1, source_target_pairs={{0,8},{1,9},{2,10},{3,11},{4,12},{5,13},{6,14},{7,15},{8,0},{9,1},... | collective-permute-start | bytes 3145736 | tf_op jit(solution)/shard_map/ppermute | solution.py:15
  179.8 0.9 copy-start
  179.8 376.8 %reduce-scatter.8.cloned.1.call-start = ((), (), s32[]{:S(2)}) async-start(), calls=%async_computation.5 | async-start | bytes 4456448 | tf_op jit(solution)/shard_map/reduce_scatter | solution.py:67
  399.3 1.4 collective-permute-start.4
  400.8 8.4 %collective-permute-start.5 = (bf16[2048,64]{0,1:T(8,128)(2,1)S(1)}, bf16[2048,64]{0,1:T(8,128)(2,1)S(1)}, u32[]{:S(2)}, u32[]{:S(2)}) collective-permute-start(bf16[2048,64]{0,1:T(8,128)(2,1)S(1)} %maximum_select_fusion.17), channel_id=1, source_target_pairs={{0,2},{1,3},{2,0},{3,1},{4,6},{5,7},{6,4},{7,5},{8,10},{9,11},{10,... | collective-permute-start | bytes 786440 | tf_op jit(solution)/shard_map/ppermute | solution.py:15
  409.4 13.2 %collective-permute-start.6 = (bf16[4096,64]{0,1:T(8,128)(2,1)S(1)}, bf16[4096,64]{0,1:T(8,128)(2,1)S(1)}, u32[]{:S(2)}, u32[]{:S(2)}) collective-permute-start(bf16[4096,64]{0,1:T(8,128)(2,1)S(1)} %maximum_select_fusion.15), channel_id=1, source_target_pairs={{0,4},{1,5},{2,6},{3,7},{4,0},{5,1},{6,2},{7,3},{8,12},{9,13},{10,... | collective-permute-start | bytes 1572872 | tf_op jit(solution)/shard_map/ppermute | solution.py:15
  422.8 46.9 %collective-permute-start.7 = (bf16[8192,64]{0,1:T(8,128)(2,1)S(1)}, bf16[8192,64]{0,1:T(8,128)(2,1)S(1)}, u32[]{:S(2)}, u32[]{:S(2)}) collective-permute-start(bf16[8192,64]{0,1:T(8,128)(2,1)S(1)} %maximum_select_fusion.13), channel_id=1, source_target_pairs={{0,8},{1,9},{2,10},{3,11},{4,12},{5,13},{6,14},{7,15},{8,0},{9,1},... | collective-permute-start | bytes 3145736 | tf_op jit(solution)/shard_map/ppermute | solution.py:15
Sparse Core Ops, SparseCore 0:
  16.9 75.0 reduce-scatter.3
  180.0 71.2 reduce-scatter.5
  486.2 70.3 reduce-scatter.7
